TPU v7x, 32 devices: a whole 2x2x4 slice. The times are simulated.
32 devices in a mesh: grp: 2 (over x), tm: 16 (over z, y, core).
Axes of the slice: x: 2, y: 2, z: 4, core: 2. Of those that a mesh axis runs over, the one named last changes fastest.
Arguments:
- queries: bfloat16 [2, 8192, 1120], P(None, ('grp', 'tm')), parts along dimension 1, may hold values from 0.19921875 to 3
- keys: bfloat16 [2, 8192, 1120], P(None, ('grp', 'tm')), parts along dimension 1, may hold values from 0.05 to 24
- values: bfloat16 [2, 8192, 1120], P(None, ('grp', 'tm')), parts along dimension 1, may hold values from -12 to 12
- timesteps: int32 [4], P('grp'), parts along dimension 0, may hold values from 0 to 19
- gate_table: float32 [20, 2240], replicated, may hold values from -3 to 3
- out_weight: bfloat16 [1120, 2240], replicated, may hold values from -0.1875 to 0.1875
- conv_weight: float32 [9, 1120], replicated, may hold values from -1.5 to 1.5
Outputs:
- update: float32 [2, 8192, 2240], P(None, ('grp', 'tm')), parts along dimension 1
- fresh_state: float32 [32, 70, 70], P('grp'), parts along dimension 0
- fresh_total: float32 [32, 70], P('grp'), parts along dimension 0
There are 2 independent parts, one for each index of `grp`. A program takes and returns all parts, laid end to end along the dimension named above; an argument that names none is the same for every part. Nothing has to cross between parts.
All inputs are finite; a program needn't handle non-finite values.
Results may differ from a plain program's by a relative error of at most 0.0003.
The roundings to bfloat16 on the way count: a program that leaves them out, or rounds other values in their place, can miss the bound.
Values may be sent and summed in bfloat16 or wider, within the bound.
A program may use at most 64 MiB of HBM per device.

v0:
```python
import jax
import jax.numpy as jnp
from jax import lax
from jax.sharding import PartitionSpec as P

NH = 16
HD = 70
COLS = 64
ROWS_DEV = 4


EXACT = lax.Precision.HIGHEST


def extended(cells, sides, width):
    for axis, dim in sides:
        count = lax.axis_size(axis)
        ends = count - 1
        head = lax.slice_in_dim(cells, 0, width, axis=dim)
        tail = lax.slice_in_dim(cells, cells.shape[dim] - width, cells.shape[dim], axis=dim)
        cells = jnp.concatenate(
            [
                lax.ppermute(tail, axis, [(i, (i + 1) % count) for i in range(ends)]),
                cells,
                lax.ppermute(head, axis, [((i + 1) % count, i) for i in range(ends)]),
            ],
            axis=dim,
        )
    return cells


def select_gate(gate_table, position):
    step_ids = jnp.arange(gate_table.shape[0], dtype=jnp.int32)
    return jnp.sum(
        jnp.where((step_ids == position)[:, None], gate_table, jnp.zeros_like(gate_table)), axis=0
    )


def key_value_state(key_rows, values):
    key_grid = key_rows.reshape(-1, NH, HD)
    value_grid = values.reshape(-1, NH, HD)
    key_state = jnp.einsum("rhd,rhe->hde", key_grid, value_grid, preferred_element_type=jnp.float32)
    key_total = jnp.sum(key_grid.astype(jnp.float32), axis=0)
    return (key_state, key_total)


def spread(queries, key_state, key_total):
    query_grid = queries.astype(jnp.float32).reshape(-1, NH, HD)
    numer = jnp.einsum("rhd,hde->rhe", query_grid, key_state, precision=EXACT)
    denom = jnp.einsum("rhd,hd->rh", query_grid, key_total, precision=EXACT)
    return (numer / denom[..., None]).reshape(query_grid.shape[0], NH * HD)


def convolve(padded, conv_weight):
    widened = jnp.pad(padded.astype(jnp.float32), ((0, 0), (1, 1), (0, 0)))
    summed = jnp.zeros((ROWS_DEV, COLS, padded.shape[-1]), jnp.float32)
    for tap_row in range(3):
        for tap_col in range(3):
            summed = (
                summed
                + widened[tap_row : tap_row + ROWS_DEV, tap_col : tap_col + COLS]
                * conv_weight[3 * tap_row + tap_col]
            )
    return summed.reshape(ROWS_DEV * COLS, padded.shape[-1])


def local(queries, keys, values, timesteps, gate_table, out_weight, conv_weight):
    channels = NH * HD
    row_count = queries.shape[1]
    total_tokens = row_count * lax.axis_size("tm")
    gates = [select_gate(gate_table, timesteps[section]) for section in range(2)]
    state_one, total_one = key_value_state(keys[0], values[0])
    fresh_state = None
    fresh_total = None
    whole_state, whole_total = lax.psum((state_one, total_one), "tm")
    state_two, total_two = key_value_state(keys[1], values[1])
    grid_one = values[0].reshape(ROWS_DEV, COLS, channels)
    rim_values = extended(grid_one, (("tm", 0),), 1)
    position = lax.axis_index("tm")
    per_frame = lax.axis_size("tm")
    upper_rim = jnp.where(position % per_frame != 0, rim_values[0], jnp.zeros_like(rim_values[0]))
    lower_rim = jnp.where(
        (position + 1) % per_frame != 0, rim_values[-1], jnp.zeros_like(rim_values[-1])
    )
    padded_one = jnp.concatenate([upper_rim[None], grid_one, lower_rim[None]], axis=0)
    mixed_one = (
        spread(queries[0], whole_state, whole_total) + convolve(padded_one, conv_weight)
    ).astype(jnp.bfloat16)
    update_one = gates[0] * jnp.dot(mixed_one, out_weight, preferred_element_type=jnp.float32)
    fresh_state, fresh_total = lax.psum((state_two, total_two), "tm")
    moved_state = whole_state - state_one + state_two
    moved_total = whole_total - total_one + total_two
    grid_two = values[1].reshape(ROWS_DEV, COLS, channels)
    padded_two = jnp.concatenate([upper_rim[None], grid_two, lower_rim[None]], axis=0)
    mixed_two = (
        spread(queries[1], moved_state, moved_total) + convolve(padded_two, conv_weight)
    ).astype(jnp.bfloat16)
    update_two = gates[1] * jnp.dot(mixed_two, out_weight, preferred_element_type=jnp.float32)
    return (
        jnp.stack([update_one, update_two]),
        fresh_state / total_tokens,
        fresh_total / total_tokens,
    )


def solution(mesh):
    placed = (
        P(None, ("grp", "tm"), None),
        P(None, ("grp", "tm"), None),
        P(None, ("grp", "tm"), None),
        P("grp"),
        P(),
        P(),
        P(),
    )
    return jax.shard_map(
        local,
        mesh=mesh,
        in_specs=placed,
        out_specs=(P(None, ("grp", "tm"), None), P("grp", None, None), P("grp", None)),
        check_vma=False,
    )
```

profile of v0, /device:TPU:0, one launch (start us, length us, event | category | flops | bytes accessed | tf_op | source)
XLA Modules:
  0.0 146.3 jit_solution(6171141517174413717)
XLA Ops:
  7.2 0.0 copy-start.2
  7.2 0.0 all-reduce.6.cloned.1.call-start
  7.2 1.3 fusion.37
  8.5 0.8 copy.36
  9.3 1.3 collective-permute-start.1
  10.6 0.8 copy.35
  11.4 3.8 %collective-permute-start = (bf16[1,64,1120]{2,1,0:T(8,128)(2,1)}, bf16[1,64,1120]{2,1,0:T(8,128)(2,1)}, u32[]{:S(2)}, u32[]{:S(2)}) collective-permute-start(bf16[1,64,1120]{2,1,0:T(8,128)(2,1)} %copy.35), channel_id=1, source_target_pairs={{0,1},{1,2},{2,3},{3,4},{4,5},{5,6},{6,7},{7,8},{8,9},{9,10},{10,1... | collective-permute-start | bytes 430088 | tf_op jit(solution)/shard_map/ppermute | solution.py:23
  15.2 0.0 copy-done.2
  15.3 0.1 fusion.38
  15.3 0.0 copy-done.1
  15.3 0.9 fusion.39
  16.2 0.2 reshape_squeeze.18
  16.4 1.2 reshape_squeeze.21
  17.6 1.0 reshape_squeeze.19
  18.6 2.2 %fusion.41 = f32[16,70,70]{2,1,0:T(8,128)} fusion(bf16[256,16,70]{0,2,1:T(8,128)(2,1)S(1)} %reshape_squeeze.18, bf16[256,16,70]{0,2,1:T(8,128)(2,1)} %reshape_squeeze.19), kind=kOutput, calls=%fused_computation.92 | convolution fusion | flops 40140800 | bytes 1460480 | tf_op jit(solution)/shard_map/rhd,rhe->hde/dot_general | solution.py:42
  20.8 0.2 reshape_squeeze.22
  20.9 1.2 fusion.43
  22.1 0.0 all-reduce.6.cloned.1.call-update
  22.1 0.4 convert_reduce_fusion.1
  22.5 0.2 copy-done.9
  22.7 0.6 fusion.40
  23.3 0.1 reduce_sum.42
  23.4 0.1 reduce_sum.45
  23.5 63.1 %all-reduce.2 = (f32[16,70]{1,0:T(8,128)S(1)}, f32[16,70]{1,0:T(8,128)S(1)}) all-reduce(f32[16,70]{1,0:T(8,128)S(1)} %reduce_sum.42, f32[16,70]{1,0:T(8,128)S(1)} %reduce_sum.45), channel_id=1, replica_groups=mesh['grp'=2,'tm'=16] {'tm'}, use_global_device_ids=true, to_apply=%region_3.4 | all-reduce | flops 2240 | bytes 17920 | tf_op jit(solution)/shard_map/psum | solution.py:75
  86.6 0.6 broadcast_multiply_fusion.1
  87.2 0.0 copy-done.7
  87.2 0.1 slice_reduce_fusion.8
  87.3 1.3 fusion.36
  88.6 0.2 reshape.51
  88.8 0.0 copy-start.3
  88.8 0.2 reshape.54
  88.9 0.0 copy-start.5
  89.0 0.4 fusion.42
  89.3 0.4 fusion.44
  89.7 0.0 copy-done.3
  89.7 1.2 iota_compare_fusion
  91.0 0.0 copy-done.5
  91.0 0.0 copy-start.6
  91.0 0.3 copy.34
  91.3 0.3 copy.37
  91.6 0.6 copy.40
  92.2 0.0 copy-done.6
  92.2 0.1 select_reduce_fusion.1
  92.4 0.0 collective-permute-done.1
  92.4 0.9 broadcast_select_fusion
  93.3 0.0 collective-permute-done
  93.4 0.3 fusion.32
  93.6 2.4 %fusion.12 = (f32[4,64,1120]{2,1,0:T(8,128)S(1)}, f32[4,64,1120]{2,1,0:T(8,128)S(1)}) fusion(f32[6,64,1120]{2,1,0:T(8,128)S(1)} %get-tuple-element.34, f32[1120]{0:T(1024)S(1)} %get-tuple-element.20, f32[1120]{0:T(1024)S(1)} %get-tuple-element.21, f32[1120]{0:T(1024)S(1)} %get-tuple-element.14, f32[1120]{0:T(1024)S(1)} %get-tuple-element.15, ...), kind=kLoop, calls=%fused_computation.29 | loop fusion | flops 9748480 | bytes 12984320 | tf_op jit(solution)/shard_map/add | solution.py:60
  96.0 0.4 copy.22
  96.4 0.0 copy-start.8
  96.4 0.4 copy.26
  96.8 22.5 %all-reduce.6.cloned.1.call-done = (f32[16,70,70]{2,1,0:T(8,128)}, f32[16,70,70]{2,1,0:T(8,128)}) async-done(((f32[16,70,70]{2,1,0:T(8,128)}, f32[16,70,70]{2,1,0:T(8,128)}), (f32[16,70,70]{2,1,0:T(8,128)}, f32[16,70,70]{2,1,0:T(8,128)})) %all-reduce.6.cloned.1.call-update) | async-done | bytes 627216 | tf_op jit(solution)/shard_map/psum | solution.py:75
  119.3 2.3 %fusion.3 = f32[256,16,70]{0,2,1:T(8,128)S(1)} fusion(bf16[256,16,70]{0,2,1:T(8,128)(2,1)} %copy-done.5, f32[256,16]{0,1:T(8,128)S(1)} %bitcast.72, f32[16,70,70]{2,1,0:T(8,128)} %fusion.43, f32[16,70,70]{2,1,0:T(8,128)} %get-tuple-element.24, f32[16,70,70]{2,1,0:T(8,128)} %fusion.41), kind=kOutput, calls=%fused_computation.20 | convolution fusion | flops 241288320 | bytes 2677504 | tf_op jit(solution)/shard_map/rhd,hde->rhe/dot_general | solution.py:49
  121.6 1.2 reshape.55
  122.7 1.2 broadcast_multiply_fusion
  123.9 0.9 copy.27
  124.9 1.7 %fusion.2 = f32[256,16,70]{0,2,1:T(8,128)} fusion(f32[16,70,70]{2,1,0:T(8,128)S(1)} %copy-done.10, bf16[256,16,70]{0,2,1:T(8,128)(2,1)S(1)} %copy-done.4, f32[256,16]{0,1:T(8,128)S(1)} %bitcast.71), kind=kOutput, calls=%fused_computation.19 | convolution fusion | flops 241131520 | bytes 2050304 | tf_op jit(solution)/shard_map/rhd,hde->rhe/dot_general | solution.py:49
  126.6 2.5 %reshape.52 = f32[256,1120]{0,1:T(8,128)} reshape(f32[256,16,70]{0,2,1:T(8,128)} %fusion.2) | data formatting | bytes 2293760 | tf_op jit(solution)/shard_map/reshape | solution.py:51
  129.0 5.4 %fusion = f32[1,256,2240]{1,2,0:T(8,128)S(1)} fusion(bf16[1120,2240]{1,0:T(8,128)(2,1)} %param.12, f32[2240]{0:T(1024)S(1)} %get-tuple-element.11, f32[256,1120]{0,1:T(8,128)} %reshape.52, f32[256,1120]{0,1:T(8,128)S(1)} %copy.22), kind=kOutput, calls=%fused_computation.3 | convolution fusion | flops 1285652480 | bytes 9614080 | tf_op jit(solution)/shard_map/dot_general | solution.py:89
  134.5 0.0 slice-done
  134.5 0.0 slice-done.1
  134.5 0.0 copy-done
  134.5 2.5 %fusion.1 = f32[1,256,2240]{1,2,0:T(8,128)S(1)} fusion(bf16[1120,2240]{1,0:T(8,128)(2,1)S(1)} %bitcast.64, f32[2240]{0:T(1024)S(1)} %get-tuple-element.12, f32[256,1120]{0,1:T(8,128)S(1)} %copy-done, f32[256,1120]{0,1:T(8,128)S(1)} %copy.26), kind=kOutput, calls=%fused_computation.4 | convolution fusion | flops 1285652480 | bytes 9614080 | tf_op jit(solution)/shard_map/dot_general | solution.py:98
  137.0 2.4 %pad_maximum_fusion = f32[2,256,2240]{1,2,0:T(8,128)} fusion(f32[1,256,2240]{1,2,0:T(8,128)S(1)} %fusion.1, f32[1,256,2240]{1,2,0:T(8,128)S(1)} %fusion), kind=kLoop, calls=%fused_computation | loop fusion | flops 1146880 | bytes 9175040 | tf_op jit(solution)/shard_map/stack | solution.py:100
  (15 shorter events, 0.1 us)
Async XLA Ops:
  7.2 8.1 %copy-start.2 = (bf16[2,256,1120]{1,2,0:T(8,128)(2,1)S(1)}, bf16[2,256,1120]{1,2,0:T(8,128)(2,1)}, u32[]{:S(2)}) copy-start(bf16[2,256,1120]{1,2,0:T(8,128)(2,1)} %param.9) | copy-start | bytes 3440644
  7.2 112.1 %all-reduce.6.cloned.1.call-start = ((), (), s32[]{:S(2)}) async-start(), calls=%async_computation | async-start | bytes 2359296 | tf_op jit(solution)/shard_map/psum | solution.py:75
  9.3 83.0 %collective-permute-start.1 = (bf16[1,64,1120]{2,1,0:T(8,128)(2,1)}, bf16[1,64,1120]{2,1,0:T(8,128)(2,1)}, u32[]{:S(2)}, u32[]{:S(2)}) collective-permute-start(bf16[1,64,1120]{2,1,0:T(8,128)(2,1)} %copy.36), channel_id=1, source_target_pairs={{1,0},{2,1},{3,2},{4,3},{5,4},{6,5},{7,6},{8,7},{9,8},{10,9},{11,1... | collective-permute-start | bytes 430088 | tf_op jit(solution)/shard_map/ppermute | solution.py:25
  11.4 3.9 %copy-start.1 = (bf16[2,256,1120]{1,2,0:T(8,128)(2,1)S(1)}, bf16[2,256,1120]{1,2,0:T(8,128)(2,1)}, u32[]{:S(2)}) copy-start(bf16[2,256,1120]{1,2,0:T(8,128)(2,1)} %param.8) | copy-start | bytes 3440644
  11.4 81.9 %collective-permute-start = (bf16[1,64,1120]{2,1,0:T(8,128)(2,1)}, bf16[1,64,1120]{2,1,0:T(8,128)(2,1)}, u32[]{:S(2)}, u32[]{:S(2)}) collective-permute-start(bf16[1,64,1120]{2,1,0:T(8,128)(2,1)} %copy.35), channel_id=1, source_target_pairs={{0,1},{1,2},{2,3},{3,4},{4,5},{5,6},{6,7},{7,8},{8,9},{9,10},{10,1... | collective-permute-start | bytes 430088 | tf_op jit(solution)/shard_map/ppermute | solution.py:23
  22.1 0.7 copy-start.9
  22.1 65.1 %copy-start.7 = (f32[9,1120]{1,0:T(8,128)S(1)}, f32[9,1120]{1,0:T(8,128)}, u32[]{:S(2)}) copy-start(f32[9,1120]{1,0:T(8,128)} %param.13) | copy-start | bytes 120964
  88.8 0.9 copy-start.3
  88.9 2.0 %copy-start.5 = (bf16[256,16,70]{0,2,1:T(8,128)(2,1)}, bf16[256,16,70]{0,2,1:T(8,128)(2,1)S(1)}, u32[]{:S(2)}) copy-start(bf16[256,16,70]{0,2,1:T(8,128)(2,1)S(1)} %reshape.54) | copy-start | bytes 1720324
  91.0 1.2 copy-start.6
  96.4 22.9 %copy-start.8 = (f32[16,1,256]{2,0,1:T(8,128)S(1)}, f32[16,1,256]{2,0,1:T(8,128)}, u32[]{:S(2)}) copy-start(f32[16,1,256]{2,0,1:T(8,128)} %copy.40) | copy-start | bytes 49156
  122.7 2.1 %copy-start.4 = (bf16[256,16,70]{0,2,1:T(8,128)(2,1)S(1)}, bf16[256,16,70]{0,2,1:T(8,128)(2,1)}, u32[]{:S(2)}) copy-start(bf16[256,16,70]{0,2,1:T(8,128)(2,1)} %copy-done.3) | copy-start | bytes 1720324
  122.7 2.1 %copy-start.10 = (f32[16,70,70]{2,1,0:T(8,128)S(1)}, f32[16,70,70]{2,1,0:T(8,128)}, u32[]{:S(2)}) copy-start(f32[16,70,70]{2,1,0:T(8,128)} %get-tuple-element.24) | copy-start | bytes 940804
  126.5 7.9 %slice-start = ((s8[5160960]{0:T(1024)(128)(4,1)}), s8[966656]{0:T(1024)(128)(4,1)S(1)}, s32[]{:S(2)}) async-start(s8[5160960]{0:T(1024)(128)(4,1)} %bitcast.63), calls=%async_computation.1 | async-start | bytes 1933312
  129.0 5.4 %slice-start.1 = ((s8[5160960]{0:T(1024)(128)(4,1)}), s8[4194304]{0:T(1024)(128)(4,1)S(1)}, s32[]{:S(2)}) async-start(s8[5160960]{0:T(1024)(128)(4,1)} %bitcast.63), calls=%async_computation.2 | async-start | bytes 8388608
  129.0 5.4 %copy-start = (f32[256,1120]{0,1:T(8,128)S(1)}, f32[256,1120]{0,1:T(8,128)}, u32[]{:S(2)}) copy-start(f32[256,1120]{0,1:T(8,128)} %reshape.55) | copy-start | bytes 3440644
Sparse Core Ops, SparseCore 0:
  22.2 96.9 all-reduce.5
where the time goes:
time: 147 us; the launch traced here: 146 us
  blocking collectives  63.1 us (43%)
  waiting for transfers between devices  22.5 us (15%)
  matrix products  16 us (11%)
  local copies, waits for them, and re-layouts  15.6 us (11%)
  between operations  14.3 us (10%)
  other arithmetic  9.62 us (7%)
  starting transfers between devices  5.13 us (3%)
    psum x1, blocking collectives, local(): whole_state, whole_total = lax.psum((state_one, total_one), 'tm')  63.1 us
    psum x1, waiting for transfers between devices, local(): whole_state, whole_total = lax.psum((state_one, total_one), 'tm')  22.5 us
    dot_general x1, matrix products, local(): jnp.dot(mixed_one, out_weight, preferred_element_type=jnp.float32)  5.41 us
    dot_general x2, matrix products, spread(): numer = jnp.einsum('rhd,hde->rhe', query_grid, key_state, precision=EXACT)  3.98 us
    ppermute x1, starting transfers between devices, extended(): lax.ppermute(tail, axis, [(i, (i + 1) % count) for i in range(ends)])  3.81 us
    reshape x2, local copies, waits for them, and re-layouts, spread(): return (numer / denom[..., None]).reshape(query_grid.shape[0], NH * HD)  3.66 us
    unnamed x31, local copies, waits for them, and re-layouts  3.45 us
    dot_general x2, matrix products, key_value_state(): jnp.einsum('rhd,rhe->hde', key_grid, value_grid, preferred_element_type=j...  3.38 us
  transfers between devices with their start and end apart: 3, of which 1 were waited for; matrix products, arithmetic and copies ran while one was open for 13% of the time, Pallas kernels for 0%

commit v1 on v0

v1 whole, which is shorter than its diff:
```python
import functools

import jax
import jax.numpy as jnp
from jax import lax
from jax.experimental import pallas as pl
from jax.experimental.pallas import tpu as pltpu
from jax.sharding import PartitionSpec as P

NH = 16
HD = 70
COLS = 64
CH = NH * HD
LT = 128
NC = -(-CH // LT)
NR = 9
MESH = pl.DeviceIdType.MESH
F32 = jnp.float32
BF16 = jnp.bfloat16


def spans(width):
    out = []
    for c0 in range(0, CH, width):
        c1 = min(c0 + width, CH)
        h0, h1 = c0 // HD, (c1 - 1) // HD
        r0 = h0 * HD // LT * LT
        r1 = min(-(-(h1 + 1) * HD // LT) * LT, CH)
        out.append((c0, c1, h0, h1, r0, r1))
    return out


def local_state(k_ref, v_ref, s, part, band, put):
    tokens = k_ref.shape[1]
    ones = jnp.ones((8, tokens), BF16)
    for c, (c0, c1, h0, h1, r0, r1) in enumerate(spans(LT)):
        w = c1 - c0
        band[0 : r1 - r0, 0:w] = lax.dot_general(
            k_ref[s, :, r0:r1], v_ref[s, :, c0:c1], (((0,), (0,)), ((), ())), preferred_element_type=F32
        )
        count = jnp.dot(ones, k_ref[s, :, c0:c1], preferred_element_type=F32)[0:1]
        lane = c0 + lax.broadcasted_iota(jnp.int32, (NR * 8, w), 1)
        row = lax.broadcasted_iota(jnp.int32, (NR * 8, w), 0)
        tile = jnp.zeros((NR * 8, w), F32)
        for h in range(h0, h1 + 1):
            rows = band[h * HD - r0 : h * HD - r0 + NR * 8, 0:w]
            tile = jnp.where((lane >= h * HD) & (lane < (h + 1) * HD), rows, tile)
        tile = jnp.where(row < HD, tile, jnp.where(row == HD, count, 0.0))
        for r in range(NR):
            put(part, s, r * NC + c, w, tile[8 * r : 8 * r + 8])


def convolve(v_ref, s, rim, cw_ref, out_ref):
    tokens = v_ref.shape[1]
    for c0, c1, *_ in spans(LT):
        w = c1 - c0
        mid = v_ref[s, :, c0:c1].astype(F32)
        pad = jnp.concatenate([rim[0, :, c0:c1].astype(F32), mid, rim[1, :, c0:c1].astype(F32)], axis=0)
        col = lax.broadcasted_iota(jnp.int32, (tokens, w), 0) % COLS
        acc = None
        for b in range(3):
            one = sum(
                pad[a * COLS : a * COLS + tokens] * cw_ref[3 * a + b : 3 * a + b + 1, c0:c1] for a in range(3)
            )
            if b == 0:
                one = jnp.where(col != 0, pltpu.roll(one, 1, 0), 0.0)
            if b == 2:
                one = jnp.where(col != COLS - 1, pltpu.roll(one, tokens - 1, 0), 0.0)
            acc = one if acc is None else acc + one
        out_ref[s, :, c0:c1] = acc


def gather_kernel(
    n, m, k_ref, v_ref, cw_ref, st_ref, conv_ref,
    part, cin, cur, rin, full, rim, band,
    core_s, core_r, p1_s, p1_r, p2_s, p2_r, fw_s, fw_r, rim_s, rim_r,
):
    me = lax.axis_index("tm")
    half = n // 2
    core = me % 2
    chip = me // 2
    mate = chip * 2 + (1 - core)
    tokens = k_ref.shape[1]

    def at(k):
        return lax.rem(chip + k, half) * 2 + core

    def place(idx):
        g, j = idx // m, idx % m
        return g // half, g % half, j

    def put(ref, s, idx, w, value):
        c, p, j = place(idx)
        ref[s, c, p, j, :, 0:w] = value

    barrier = pltpu.get_barrier_semaphore()
    pl.semaphore_signal(barrier, inc=1, device_id={"tm": mate}, device_id_type=MESH)
    for k in range(1, half):
        pl.semaphore_signal(barrier, inc=1, device_id={"tm": at(k)}, device_id_type=MESH)
    beside = lax.rem(me + 2 * core - 1 + n, n)
    pl.semaphore_signal(barrier, inc=1, device_id={"tm": beside}, device_id_type=MESH)
    pl.semaphore_wait(barrier, half + 1)

    def remote(src, dst, ss, rs, dev):
        return pltpu.make_async_remote_copy(
            src_ref=src, dst_ref=dst, send_sem=ss, recv_sem=rs, device_id={"tm": dev}, device_id_type=MESH
        )

    def swap(s):
        return remote(part.at[s, 1 - core], cin.at[s], core_s.at[s], core_r.at[s], mate)

    def first(s, k):
        return remote(cur.at[s, lax.rem(chip + k, half)], rin.at[s, k], p1_s.at[s, k], p1_r.at[s, k], at(k))

    def second(s, k):
        return remote(
            full.at[s, core, chip], full.at[s, core, chip], p2_s.at[s, k], p2_r.at[s, k], at(k)
        )

    def second_in(s, k):
        src = lax.rem(chip + half - k, half)
        return remote(full.at[s, core, src], full.at[s, core, src], p2_s.at[s, k], p2_r.at[s, k], at(k))

    def onward(s, k):
        src = lax.rem(chip + half - k, half)
        return remote(full.at[s, core, src], full.at[s, core, src], fw_s.at[s, k], fw_r.at[s, k], mate)

    def onward_in(s, k):
        src = lax.rem(chip + half - k, half)
        return remote(full.at[s, 1 - core, src], full.at[s, 1 - core, src], fw_s.at[s, k], fw_r.at[s, k], mate)

    down = remote(v_ref.at[0, pl.ds(tokens - COLS, COLS)], rim.at[0], rim_s.at[0], rim_r.at[0], me + 1)
    up = remote(v_ref.at[0, pl.ds(0, COLS)], rim.at[1], rim_s.at[1], rim_r.at[1], me - 1)

    part[...] = jnp.zeros_like(part)
    local_state(k_ref, v_ref, 0, part, band, put)
    swap(0).start()

    @pl.when(me < n - 1)
    def _():
        down.start()

    @pl.when(me > 0)
    def _():
        up.start()

    local_state(k_ref, v_ref, 1, part, band, put)
    swap(1).start()
    for s in range(2):
        swap(s).wait()
        cur[s] = part[s, core] + cin[s]
        for k in range(1, half):
            first(s, k).start()

    @pl.when(me == 0)
    def _():
        rim[0] = jnp.zeros_like(rim[0])

    @pl.when(me == n - 1)
    def _():
        rim[1] = jnp.zeros_like(rim[1])

    @pl.when(me < n - 1)
    def _():
        down.wait_send()
        up.wait_recv()

    @pl.when(me > 0)
    def _():
        up.wait_send()
        down.wait_recv()

    for s in range(2):
        convolve(v_ref, s, rim, cw_ref, conv_ref)
        total = cur[s, chip]
        for k in range(1, half):
            first(s, k).wait()
            total = total + rin[s, k]
        full[s, core, chip] = total
        for k in range(1, half):
            second(s, k).start()
        onward(s, 0).start()
    for s in range(2):
        for k in range(1, half):
            second_in(s, k).wait_recv()
            onward(s, k).start()
        for k in range(1, half):
            second(s, k).wait_send()
    for s in range(2):
        for k in range(half):
            onward(s, k).wait_send()
            onward_in(s, k).wait_recv()
    for r in range(NR):
        for c in range(NC):
            where = place(r * NC + c)
            rows, cols = slice(8 * r, 8 * r + 8), slice(LT * c, LT * c + LT)
            whole = full[(0, *where)]
            st_ref[0, rows, cols] = whole
            st_ref[1, rows, cols] = whole - part[(0, *where)] + part[(1, *where)]
            st_ref[2, rows, cols] = full[(1, *where)]


def split(x):
    high = x.astype(BF16)
    return high, (x - high.astype(F32)).astype(BF16)


def mix(q_ref, st_ref, conv_ref, s, mixed, block):
    tokens = q_ref.shape[1]
    for c0, c1, h0, h1, r0, r1 in spans(256):
        w, depth = c1 - c0, r1 - r0
        block[...] = jnp.zeros_like(block)
        state = st_ref[s, 0:72, c0:c1]
        lane = c0 + lax.broadcasted_iota(jnp.int32, (HD, w), 1)
        for h in range(h0, h1 + 1):
            block[h * HD - r0 : (h + 1) * HD - r0, 0:w] = jnp.where(
                (lane >= h * HD) & (lane < (h + 1) * HD), state[0:HD], 0.0
            )
        high, low = split(block[0:depth, 0:w])
        query = q_ref[s, :, r0:r1]
        numer = jnp.dot(query, high, preferred_element_type=F32) + jnp.dot(
            query, low, preferred_element_type=F32
        )
        row_head = jnp.floor((lax.broadcasted_iota(jnp.int32, (depth, w), 0).astype(F32) + (r0 + 0.5)) / HD)
        col_head = jnp.floor((lax.broadcasted_iota(jnp.int32, (depth, w), 1).astype(F32) + (c0 + 0.5)) / HD)
        same = (row_head == col_head).astype(F32).astype(BF16)
        high, low = split(query.astype(F32) * st_ref[s, HD : HD + 1, r0:r1])
        denom = jnp.dot(high, same, preferred_element_type=F32) + jnp.dot(low, same, preferred_element_type=F32)
        mixed[s * tokens : (s + 1) * tokens, c0:c1] = (numer / denom + conv_ref[s, :, c0:c1]).astype(BF16)


def project_kernel(
    total_tokens, ts_ref, q_ref, st_ref, conv_ref, gate_ref, w_ref, out_ref, fs_ref, ft_ref, mixed, block
):
    tokens = q_ref.shape[1]

    @pl.when(pl.program_id(0) == 0)
    def _():
        for s in range(2):
            mix(q_ref, st_ref, conv_ref, s, mixed, block)
        for h in range(NH):
            base = min(h * HD // LT * LT, NC * LT - 2 * LT)
            both = st_ref[2, :, base : base + 2 * LT] / total_tokens
            both = pltpu.roll(both, (2 * LT - (h * HD - base)) % (2 * LT), 1)
            fs_ref[h] = both[0:HD, 0:HD]
            ft_ref[h : h + 1, :] = both[HD : HD + 1, 0:HD]

    for s in range(2):
        acc = jnp.dot(mixed[s * tokens : (s + 1) * tokens, :], w_ref[...], preferred_element_type=F32)
        out_ref[s] = gate_ref[pl.ds(ts_ref[s], 1), :] * acc


def local(n, queries, keys, values, timesteps, gate_table, out_weight, conv_weight):
    tokens = queries.shape[1]
    width = out_weight.shape[1]
    half = n // 2
    m = -(-NR * NC // n)
    vmem = pl.BlockSpec(memory_space=pltpu.VMEM)
    dma = pltpu.SemaphoreType.DMA
    states, conv = pl.pallas_call(
        functools.partial(gather_kernel, n, m),
        out_shape=(
            jax.ShapeDtypeStruct((3, NR * 8, NC * LT), F32),
            jax.ShapeDtypeStruct((2, tokens, CH), F32),
        ),
        in_specs=[vmem] * 3,
        out_specs=(vmem, vmem),
        scratch_shapes=[
            pltpu.VMEM((2, 2, half, m, 8, LT), F32),
            pltpu.VMEM((2, half, m, 8, LT), F32),
            pltpu.VMEM((2, half, m, 8, LT), F32),
            pltpu.VMEM((2, half, m, 8, LT), F32),
            pltpu.VMEM((2, 2, half, m, 8, LT), F32),
            pltpu.VMEM((2, COLS, CH), BF16),
            pltpu.VMEM((640, LT), F32),
            dma((2,)), dma((2,)),
            dma((2, half)), dma((2, half)),
            dma((2, half)), dma((2, half)),
            dma((2, half)), dma((2, half)),
            dma((2,)), dma((2,)),
        ],
        compiler_params=pltpu.CompilerParams(
            collective_id=0, has_side_effects=True, vmem_limit_bytes=40 * 2**20
        ),
        name="states",
    )(keys, values, conv_weight)
    nb = 640
    once = lambda shape: pl.BlockSpec(shape, lambda i, ts: (0,) * len(shape), pipeline_mode=pl.Buffered(1))
    return pl.pallas_call(
        functools.partial(project_kernel, float(tokens * n)),
        out_shape=(
            jax.ShapeDtypeStruct((2, tokens, width), F32),
            jax.ShapeDtypeStruct((NH, HD, HD), F32),
            jax.ShapeDtypeStruct((NH, HD), F32),
        ),
        grid_spec=pltpu.PrefetchScalarGridSpec(
            num_scalar_prefetch=1,
            grid=(pl.cdiv(width, nb),),
            in_specs=[
                once((2, tokens, CH)),
                once((3, NR * 8, NC * LT)),
                once((2, tokens, CH)),
                pl.BlockSpec((gate_table.shape[0], nb), lambda i, ts: (0, i)),
                pl.BlockSpec((CH, nb), lambda i, ts: (0, i)),
            ],
            out_specs=(
                pl.BlockSpec((2, tokens, nb), lambda i, ts: (0, 0, i)),
                pl.BlockSpec((NH, HD, HD), lambda i, ts: (0, 0, 0)),
                pl.BlockSpec((NH, HD), lambda i, ts: (0, 0)),
            ),
            scratch_shapes=[pltpu.VMEM((2 * tokens, CH), BF16), pltpu.VMEM((640, 256), F32)],
        ),
        compiler_params=pltpu.CompilerParams(
            dimension_semantics=("arbitrary",), vmem_limit_bytes=40 * 2**20
        ),
        name="project",
    )(timesteps, queries, states, conv, gate_table, out_weight)


def solution(mesh):
    n = mesh.shape["tm"]
    placed = (
        P(None, ("grp", "tm"), None),
        P(None, ("grp", "tm"), None),
        P(None, ("grp", "tm"), None),
        P("grp"),
        P(),
        P(),
        P(),
    )
    return jax.shard_map(
        functools.partial(local, n),
        mesh=mesh,
        in_specs=placed,
        out_specs=(P(None, ("grp", "tm"), None), P("grp", None, None), P("grp", None)),
        check_vma=False,
    )
```

time: 147 us -> 54.3 us (0.37)
  blocking collectives: 63.1 us -> 0 us
  Pallas kernels: 0 us -> 39.2 us
  waiting for transfers between devices: 22.5 us -> 0 us
  matrix products: 16 us -> 0 us
  between operations: 14.3 us -> 0.7 us
  other arithmetic: 9.62 us -> 0 us
  starting transfers between devices: 5.13 us -> 0 us
  local copies, waits for them, and re-layouts: 15.6 us -> 14.1 us
    psum x1 -> x0, blocking collectives: 63.1 us -> none  [local(): whole_state, whole_total = lax.psum((state_one, total_one), 'tm')]
    pallas_call x0 -> x2, Pallas kernels: none -> 39.2 us  [the longest x1 28.6 us: local(): pl.pallas_call(functools.partial(gather_kernel, n, m), out_shape=(jax.Sha...]
    psum x1 -> x0, waiting for transfers between devices: 22.5 us -> none  [local(): whole_state, whole_total = lax.psum((state_one, total_one), 'tm')]
    dot_general x8 -> x0, matrix products: 16 us -> none  [the longest x1 5.41 us: local(): jnp.dot(mixed_one, out_weight, preferred_element_type=jnp.float32)]
    pallas_call x0 -> x2, local copies, waits for them, and re-layouts: none -> 6.92 us  [local(): pl.pallas_call(functools.partial(project_kernel, float(tokens * n)), out_...]
    ppermute x2 -> x0, starting transfers between devices: 5.09 us -> none  [the longest x1 3.81 us: extended(): lax.ppermute(tail, axis, [(i, (i + 1) % count) for i in range(ends)])]
    reshape x6 -> x0, local copies, waits for them, and re-layouts: 4.68 us -> none  [the longest x2 3.66 us: spread(): return (numer / denom[..., None]).reshape(query_grid.shape[0], NH * HD)]
    slice x6 -> x0, local copies, waits for them, and re-layouts: 4.24 us -> none  [the longest x1 1.31 us: local(): queries[0]]
  transfers between devices with their start and end apart: 3 -> 0, of which waited for: 1 -> 0; matrix products, arithmetic and copies ran while one was open for 13% -> 0% of each run, Pallas kernels for 0% -> 0%
where the time goes in v1:
time: 54.3 us; the launch traced here: 54 us
  Pallas kernels  39.2 us (72%)
  local copies, waits for them, and re-layouts  14.1 us (26%)
  between operations  0.7 us (1%)
    pallas_call x1, Pallas kernels, local(): pl.pallas_call(functools.partial(gather_kernel, n, m), out_shape=(jax.Sha...  28.6 us
    pallas_call x1, Pallas kernels, local(): pl.pallas_call(functools.partial(project_kernel, float(tokens * n)), out_...  10.6 us
    unnamed x13, local copies, waits for them, and re-layouts  7.16 us
    pallas_call x2, local copies, waits for them, and re-layouts, local(): pl.pallas_call(functools.partial(project_kernel, float(tokens * n)), out_...  6.92 us

profile of v1, /device:TPU:0, one launch (start us, length us, event | category | flops | bytes accessed | tf_op | source)
XLA Modules:
  0.0 54.0 jit_solution(84592836960456155)
XLA Ops:
  0.6 0.0 copy-start.4
  0.6 1.8 %copy.12.q_ref = bf16[2,256,1120]{2,1,0:T(8,128)(2,1)S(1)} copy(bf16[2,256,1120]{1,2,0:T(8,128)(2,1)} %param.7) | data formatting | bytes 2293760 | tf_op args[0]
  2.4 0.0 copy-done.4
  2.4 0.7 %copy.10.k_ref = bf16[2,256,1120]{2,1,0:T(8,128)(2,1)S(1)} copy(bf16[2,256,1120]{1,2,0:T(8,128)(2,1)S(1)} %copy-done.4) | data formatting | bytes 2293760 | tf_op args[1]
  3.1 1.7 %copy.11.v_ref = bf16[2,256,1120]{2,1,0:T(8,128)(2,1)S(1)} copy(bf16[2,256,1120]{1,2,0:T(8,128)(2,1)} %param.9) | data formatting | bytes 2293760 | tf_op args[2]
  4.8 0.0 copy-start.2
  4.8 0.9 %copy-done.2 = f32[9,1120]{1,0:T(8,128)S(1)} copy-done((f32[9,1120]{1,0:T(8,128)S(1)}, f32[9,1120]{1,0:T(8,128)}, u32[]{:S(2)}) %copy-start.2) | copy-done | bytes 40344
  5.7 0.0 copy-start.1
  5.7 0.0 copy-start.3
  5.7 28.6 %states.1 = (f32[3,72,1152]{2,1,0:T(8,128)S(1)}, f32[2,256,1120]{2,1,0:T(8,128)S(1)}) custom-call(bf16[2,256,1120]{2,1,0:T(8,128)(2,1)S(1)} %copy.10.k_ref, bf16[2,256,1120]{2,1,0:T(8,128)(2,1)S(1)} %copy.11.v_ref, f32[9,1120]{1,0:T(8,128)S(1)} %copy-done.2), custom_call_target="tpu_custom_call" | custom-call | tf_op jit(solution)/shard_map/states/pallas_call | solution.py:260
  34.3 0.0 copy-done.1
  34.3 0.0 copy-done.3
  34.3 10.6 %project.1 = (f32[2,256,2240]{2,1,0:T(8,128)S(1)}, f32[16,70,70]{2,1,0:T(8,128)S(1)}, f32[16,70]{1,0:T(8,128)}) custom-call(s32[2]{0:T(128)S(1)} %copy-done.3, bf16[2,256,1120]{2,1,0:T(8,128)(2,1)S(1)} %copy.12.q_ref, f32[3,72,1152]{2,1,0:T(8,128)S(1)} %get-tuple-element.5.st_ref, f32[2,256,1120]{2,1,0:T(8,128)S(1)} %get-tuple-element.6.conv_ref, ...), custom_call_target="tpu_custom_call" | custom-call | tf_op jit(solution)/shard_map/project/pallas_call | solution.py:289
  45.0 0.0 copy-start
  45.0 2.1 %copy-done = f32[2,256,2240]{2,1,0:T(8,128)} copy-done((f32[2,256,2240]{2,1,0:T(8,128)}, f32[2,256,2240]{2,1,0:T(8,128)S(1)}, u32[]{:S(2)}) %copy-start) | copy-done | bytes 4587544
  47.1 6.0 %copy.13 = f32[2,256,2240]{1,2,0:T(8,128)} copy(f32[2,256,2240]{2,1,0:T(8,128)} %copy-done) | data formatting | bytes 9175040 | tf_op jit(solution)/shard_map/project/pallas_call | solution.py:289
  53.1 0.9 %copy.14 = f32[16,70,70]{2,0,1:T(8,128)} copy(f32[16,70,70]{2,1,0:T(8,128)S(1)} %get-tuple-element.8) | data formatting | bytes 627200 | tf_op jit(solution)/shard_map/project/pallas_call | solution.py:289
Async XLA Ops:
  0.6 1.8 %copy-start.4 = (bf16[2,256,1120]{1,2,0:T(8,128)(2,1)S(1)}, bf16[2,256,1120]{1,2,0:T(8,128)(2,1)}, u32[]{:S(2)}) copy-start(bf16[2,256,1120]{1,2,0:T(8,128)(2,1)} %param.8) | copy-start | bytes 3440644
  4.8 0.9 %copy-start.2 = (f32[9,1120]{1,0:T(8,128)S(1)}, f32[9,1120]{1,0:T(8,128)}, u32[]{:S(2)}) copy-start(f32[9,1120]{1,0:T(8,128)} %cw_ref.1) | copy-start | bytes 120964
  5.7 28.6 %copy-start.1 = (f32[20,2240]{1,0:T(8,128)S(1)}, f32[20,2240]{1,0:T(8,128)}, u32[]{:S(2)}) copy-start(f32[20,2240]{1,0:T(8,128)} %gate_ref.1) | copy-start | bytes 537604
  5.7 28.6 %copy-start.3 = (s32[2]{0:T(128)S(1)}, s32[2]{0:T(128)}, u32[]{:S(2)}) copy-start(s32[2]{0:T(128)} %ts_ref.1) | copy-start | bytes 28
  45.0 2.1 %copy-start = (f32[2,256,2240]{2,1,0:T(8,128)}, f32[2,256,2240]{2,1,0:T(8,128)S(1)}, u32[]{:S(2)}) copy-start(f32[2,256,2240]{2,1,0:T(8,128)S(1)} %get-tuple-element.7) | copy-start | bytes 13762564

commit v2 on v1

--- a/solution.py
+++ b/solution.py
@@ -31,14 +31,14 @@
 
 
 def local_state(k_ref, v_ref, s, part, band, put):
-    tokens = k_ref.shape[1]
-    ones = jnp.ones((8, tokens), BF16)
+    ones = jnp.ones((8, k_ref.shape[2]), BF16)
+    lanes = (((1,), (1,)), ((), ()))
     for c, (c0, c1, h0, h1, r0, r1) in enumerate(spans(LT)):
         w = c1 - c0
         band[0 : r1 - r0, 0:w] = lax.dot_general(
-            k_ref[s, :, r0:r1], v_ref[s, :, c0:c1], (((0,), (0,)), ((), ())), preferred_element_type=F32
-        )
-        count = jnp.dot(ones, k_ref[s, :, c0:c1], preferred_element_type=F32)[0:1]
+            k_ref[s, r0:r1, :], v_ref[s, c0:c1, :], lanes, preferred_element_type=F32
+        )
+        count = lax.dot_general(ones, k_ref[s, c0:c1, :], lanes, preferred_element_type=F32)[0:1]
         lane = c0 + lax.broadcasted_iota(jnp.int32, (NR * 8, w), 1)
         row = lax.broadcasted_iota(jnp.int32, (NR * 8, w), 0)
         tile = jnp.zeros((NR * 8, w), F32)
@@ -50,29 +50,52 @@
             put(part, s, r * NC + c, w, tile[8 * r : 8 * r + 8])
 
 
-def convolve(v_ref, s, rim, cw_ref, out_ref):
-    tokens = v_ref.shape[1]
-    for c0, c1, *_ in spans(LT):
-        w = c1 - c0
-        mid = v_ref[s, :, c0:c1].astype(F32)
-        pad = jnp.concatenate([rim[0, :, c0:c1].astype(F32), mid, rim[1, :, c0:c1].astype(F32)], axis=0)
-        col = lax.broadcasted_iota(jnp.int32, (tokens, w), 0) % COLS
+def pack(v_ref, lower, out_ref):
+    base = v_ref.shape[2] - LT if lower else 0
+    lane = lax.broadcasted_iota(jnp.int32, (CH // 2, LT), 1)
+    one = v_ref[0, 0 : CH // 2, base : base + LT].astype(F32)
+    two = pltpu.roll(v_ref[0, CH // 2 : CH, base : base + LT].astype(F32), LT // 2, 1)
+    keep = lane >= LT // 2 if lower else lane < LT // 2
+    out_ref[...] = jnp.where(keep, one, two).astype(BF16)
+
+
+def unpack(rim_ref, rims):
+    lane_block = rim_ref[...].astype(F32)
+    rims[0 : CH // 2] = pltpu.roll(lane_block, LT // 2, 1)
+    rims[CH // 2 : CH] = lane_block
+
+
+def convolve(v_ref, s, above, below, taps, out_ref):
+    tokens = v_ref.shape[2]
+    step = CH // 10
+    lane = lax.broadcasted_iota(jnp.int32, (step, tokens), 1)
+    col = lane % COLS
+    for c0 in range(0, CH, step):
+        mid = v_ref[s, c0 : c0 + step, :].astype(F32)
+        top = above[c0 : c0 + step, :]
+        low = below[c0 : c0 + step, :]
+        blank = jnp.zeros((step, tokens - LT), F32)
+        rows = (
+            jnp.where(lane < COLS, jnp.concatenate([top, blank], axis=1), pltpu.roll(mid, COLS, 1)),
+            mid,
+            jnp.where(
+                lane >= tokens - COLS, jnp.concatenate([blank, low], axis=1), pltpu.roll(mid, tokens - COLS, 1)
+            ),
+        )
         acc = None
         for b in range(3):
-            one = sum(
-                pad[a * COLS : a * COLS + tokens] * cw_ref[3 * a + b : 3 * a + b + 1, c0:c1] for a in range(3)
-            )
+            one = sum(rows[a] * taps[c0 : c0 + step, 3 * a + b : 3 * a + b + 1] for a in range(3))
             if b == 0:
-                one = jnp.where(col != 0, pltpu.roll(one, 1, 0), 0.0)
+                one = jnp.where(col != 0, pltpu.roll(one, 1, 1), 0.0)
             if b == 2:
-                one = jnp.where(col != COLS - 1, pltpu.roll(one, tokens - 1, 0), 0.0)
+                one = jnp.where(col != COLS - 1, pltpu.roll(one, tokens - 1, 1), 0.0)
             acc = one if acc is None else acc + one
-        out_ref[s, :, c0:c1] = acc
+        out_ref[s, c0 : c0 + step, :] = acc
 
 
 def gather_kernel(
     n, m, k_ref, v_ref, cw_ref, st_ref, conv_ref,
-    part, cin, cur, rin, full, rim, band,
+    part, cin, cur, rin, full, edge, rim, above, below, wide, taps, band,
     core_s, core_r, p1_s, p1_r, p2_s, p2_r, fw_s, fw_r, rim_s, rim_r,
 ):
     me = lax.axis_index("tm")
@@ -80,7 +103,6 @@
     core = me % 2
     chip = me // 2
     mate = chip * 2 + (1 - core)
-    tokens = k_ref.shape[1]
 
     def at(k):
         return lax.rem(chip + k, half) * 2 + core
@@ -129,12 +151,14 @@
         src = lax.rem(chip + half - k, half)
         return remote(full.at[s, 1 - core, src], full.at[s, 1 - core, src], fw_s.at[s, k], fw_r.at[s, k], mate)
 
-    down = remote(v_ref.at[0, pl.ds(tokens - COLS, COLS)], rim.at[0], rim_s.at[0], rim_r.at[0], me + 1)
-    up = remote(v_ref.at[0, pl.ds(0, COLS)], rim.at[1], rim_s.at[1], rim_r.at[1], me - 1)
+    down = remote(edge.at[0], rim.at[0], rim_s.at[0], rim_r.at[0], me + 1)
+    up = remote(edge.at[1], rim.at[1], rim_s.at[1], rim_r.at[1], me - 1)
 
     part[...] = jnp.zeros_like(part)
     local_state(k_ref, v_ref, 0, part, band, put)
     swap(0).start()
+    pack(v_ref, True, edge.at[0])
+    pack(v_ref, False, edge.at[1])
 
     @pl.when(me < n - 1)
     def _():
@@ -146,6 +170,10 @@
 
     local_state(k_ref, v_ref, 1, part, band, put)
     swap(1).start()
+    wide[...] = jnp.zeros_like(wide)
+    wide[0:9, 0:CH] = cw_ref[...]
+    for c in range(NC):
+        taps[LT * c : LT * c + LT, :] = jnp.transpose(wide[:, LT * c : LT * c + LT])
     for s in range(2):
         swap(s).wait()
         cur[s] = part[s, core] + cin[s]
@@ -170,8 +198,10 @@
         up.wait_send()
         down.wait_recv()
 
-    for s in range(2):
-        convolve(v_ref, s, rim, cw_ref, conv_ref)
+    unpack(rim.at[0], above)
+    unpack(rim.at[1], below)
+    for s in range(2):
+        convolve(v_ref, s, above, below, taps, conv_ref)
         total = cur[s, chip]
         for k in range(1, half):
             first(s, k).wait()
@@ -206,7 +236,8 @@
 
 
 def mix(q_ref, st_ref, conv_ref, s, mixed, block):
-    tokens = q_ref.shape[1]
+    tokens = q_ref.shape[2]
+    firsts = (((0,), (0,)), ((), ()))
     for c0, c1, h0, h1, r0, r1 in spans(256):
         w, depth = c1 - c0, r1 - r0
         block[...] = jnp.zeros_like(block)
@@ -216,23 +247,21 @@
             block[h * HD - r0 : (h + 1) * HD - r0, 0:w] = jnp.where(
                 (lane >= h * HD) & (lane < (h + 1) * HD), state[0:HD], 0.0
             )
-        high, low = split(block[0:depth, 0:w])
-        query = q_ref[s, :, r0:r1]
-        numer = jnp.dot(query, high, preferred_element_type=F32) + jnp.dot(
-            query, low, preferred_element_type=F32
-        )
-        row_head = jnp.floor((lax.broadcasted_iota(jnp.int32, (depth, w), 0).astype(F32) + (r0 + 0.5)) / HD)
-        col_head = jnp.floor((lax.broadcasted_iota(jnp.int32, (depth, w), 1).astype(F32) + (c0 + 0.5)) / HD)
-        same = (row_head == col_head).astype(F32).astype(BF16)
-        high, low = split(query.astype(F32) * st_ref[s, HD : HD + 1, r0:r1])
-        denom = jnp.dot(high, same, preferred_element_type=F32) + jnp.dot(low, same, preferred_element_type=F32)
-        mixed[s * tokens : (s + 1) * tokens, c0:c1] = (numer / denom + conv_ref[s, :, c0:c1]).astype(BF16)
+        query = q_ref[s, r0:r1, :]
+        numer = sum(
+            lax.dot_general(x, query, firsts, preferred_element_type=F32) for x in split(block[0:depth, 0:w])
+        )
+        row_head = jnp.floor((lax.broadcasted_iota(jnp.int32, (w, depth), 0).astype(F32) + (c0 + 0.5)) / HD)
+        col_head = jnp.floor((lax.broadcasted_iota(jnp.int32, (w, depth), 1).astype(F32) + (r0 + 0.5)) / HD)
+        norm = jnp.where(row_head == col_head, st_ref[s, HD : HD + 1, r0:r1], 0.0)
+        denom = sum(jnp.dot(x, query, preferred_element_type=F32) for x in split(norm))
+        mixed[c0:c1, s * tokens : (s + 1) * tokens] = (numer / denom + conv_ref[s, c0:c1, :]).astype(BF16)
 
 
 def project_kernel(
-    total_tokens, ts_ref, q_ref, st_ref, conv_ref, gate_ref, w_ref, out_ref, fs_ref, ft_ref, mixed, block
+    total_tokens, ts_ref, q_ref, st_ref, conv_ref, gate_ref, w_ref, out_ref, fs_ref, ft_ref, mixed, block, gates
 ):
-    tokens = q_ref.shape[1]
+    tokens = q_ref.shape[2]
 
     @pl.when(pl.program_id(0) == 0)
     def _():
@@ -246,14 +275,19 @@
             ft_ref[h : h + 1, :] = both[HD : HD + 1, 0:HD]
 
     for s in range(2):
-        acc = jnp.dot(mixed[s * tokens : (s + 1) * tokens, :], w_ref[...], preferred_element_type=F32)
-        out_ref[s] = gate_ref[pl.ds(ts_ref[s], 1), :] * acc
+        gates[s : s + 1, :] = gate_ref[pl.ds(ts_ref[s], 1), :]
+    acc = lax.dot_general(w_ref[...], mixed[...], (((0,), (0,)), ((), ())), preferred_element_type=F32)
+    for c in range(0, acc.shape[0], LT):
+        gate = jnp.transpose(gates[:, c : c + LT])
+        for s in range(2):
+            out_ref[s, c : c + LT, :] = gate[:, s : s + 1] * acc[c : c + LT, s * tokens : (s + 1) * tokens]
 
 
 def local(n, queries, keys, values, timesteps, gate_table, out_weight, conv_weight):
     tokens = queries.shape[1]
     width = out_weight.shape[1]
     half = n // 2
+    queries, keys, values = (jnp.swapaxes(x, 1, 2) for x in (queries, keys, values))
     m = -(-NR * NC // n)
     vmem = pl.BlockSpec(memory_space=pltpu.VMEM)
     dma = pltpu.SemaphoreType.DMA
@@ -261,7 +295,7 @@
         functools.partial(gather_kernel, n, m),
         out_shape=(
             jax.ShapeDtypeStruct((3, NR * 8, NC * LT), F32),
-            jax.ShapeDtypeStruct((2, tokens, CH), F32),
+            jax.ShapeDtypeStruct((2, CH, tokens), F32),
         ),
         in_specs=[vmem] * 3,
         out_specs=(vmem, vmem),
@@ -271,7 +305,12 @@
             pltpu.VMEM((2, half, m, 8, LT), F32),
             pltpu.VMEM((2, half, m, 8, LT), F32),
             pltpu.VMEM((2, 2, half, m, 8, LT), F32),
-            pltpu.VMEM((2, COLS, CH), BF16),
+            pltpu.VMEM((2, CH // 2, LT), BF16),
+            pltpu.VMEM((2, CH // 2, LT), BF16),
+            pltpu.VMEM((CH, LT), F32),
+            pltpu.VMEM((CH, LT), F32),
+            pltpu.VMEM((LT, NC * LT), F32),
+            pltpu.VMEM((NC * LT, LT), F32),
             pltpu.VMEM((640, LT), F32),
             dma((2,)), dma((2,)),
             dma((2, half)), dma((2, half)),
@@ -280,16 +319,16 @@
             dma((2,)), dma((2,)),
         ],
         compiler_params=pltpu.CompilerParams(
-            collective_id=0, has_side_effects=True, vmem_limit_bytes=40 * 2**20
+            collective_id=0, has_side_effects=True, vmem_limit_bytes=20 * 2**20
         ),
         name="states",
     )(keys, values, conv_weight)
     nb = 640
     once = lambda shape: pl.BlockSpec(shape, lambda i, ts: (0,) * len(shape), pipeline_mode=pl.Buffered(1))
-    return pl.pallas_call(
+    update, fresh, total = pl.pallas_call(
         functools.partial(project_kernel, float(tokens * n)),
         out_shape=(
-            jax.ShapeDtypeStruct((2, tokens, width), F32),
+            jax.ShapeDtypeStruct((2, width, tokens), F32),
             jax.ShapeDtypeStruct((NH, HD, HD), F32),
             jax.ShapeDtypeStruct((NH, HD), F32),
         ),
@@ -297,24 +336,29 @@
             num_scalar_prefetch=1,
             grid=(pl.cdiv(width, nb),),
             in_specs=[
-                once((2, tokens, CH)),
+                once((2, CH, tokens)),
                 once((3, NR * 8, NC * LT)),
-                once((2, tokens, CH)),
+                once((2, CH, tokens)),
                 pl.BlockSpec((gate_table.shape[0], nb), lambda i, ts: (0, i)),
                 pl.BlockSpec((CH, nb), lambda i, ts: (0, i)),
             ],
             out_specs=(
-                pl.BlockSpec((2, tokens, nb), lambda i, ts: (0, 0, i)),
+                pl.BlockSpec((2, nb, tokens), lambda i, ts: (0, i, 0)),
                 pl.BlockSpec((NH, HD, HD), lambda i, ts: (0, 0, 0)),
                 pl.BlockSpec((NH, HD), lambda i, ts: (0, 0)),
             ),
-            scratch_shapes=[pltpu.VMEM((2 * tokens, CH), BF16), pltpu.VMEM((640, 256), F32)],
+            scratch_shapes=[
+                pltpu.VMEM((CH, 2 * tokens), BF16),
+                pltpu.VMEM((640, 256), F32),
+                pltpu.VMEM((LT, nb), F32),
+            ],
         ),
         compiler_params=pltpu.CompilerParams(
-            dimension_semantics=("arbitrary",), vmem_limit_bytes=40 * 2**20
+            dimension_semantics=("arbitrary",), vmem_limit_bytes=28 * 2**20
         ),
         name="project",
     )(timesteps, queries, states, conv, gate_table, out_weight)
+    return jnp.swapaxes(update, 1, 2), fresh, total
 
 
 def solution(mesh):

time: 54.3 us -> 45.7 us (0.84)
  local copies, waits for them, and re-layouts: 14.1 us -> 6.87 us
  Pallas kernels: 39.2 us -> 37.6 us
    pallas_call x2 -> x0, local copies, waits for them, and re-layouts: 6.92 us -> none  [local(): pl.pallas_call(functools.partial(project_kernel, float(tokens * n)), out_...]
    pallas_call x1, Pallas kernels: 10.6 us -> 9.24 us  [local(): pl.pallas_call(functools.partial(project_kernel, float(tokens * n)), out_...]
    unnamed x13 -> x15, local copies, waits for them, and re-layouts: 7.16 us -> 6.87 us
where the time goes in v2:
time: 45.7 us; the launch traced here: 45.2 us
  Pallas kernels  37.6 us (82%)
  local copies, waits for them, and re-layouts  6.87 us (15%)
  between operations  0.69 us (2%)
    pallas_call x1, Pallas kernels, local(): pl.pallas_call(functools.partial(gather_kernel, n, m), out_shape=(jax.Sha...  28.4 us
    pallas_call x1, Pallas kernels, local(): pl.pallas_call(functools.partial(project_kernel, float(tokens * n)), out_...  9.24 us
    unnamed x15, local copies, waits for them, and re-layouts  6.87 us

profile of v2, /device:TPU:0, one launch (start us, length us, event | category | flops | bytes accessed | tf_op | source)
XLA Modules:
  0.0 45.2 jit_solution(4371953993126099627)
XLA Ops:
  0.6 0.0 copy-start.1
  0.6 0.0 copy-start.2
  0.7 1.3 %copy-done.2 = bf16[2,256,1120]{1,2,0:T(8,128)(2,1)S(1)} copy-done((bf16[2,256,1120]{1,2,0:T(8,128)(2,1)S(1)}, bf16[2,256,1120]{1,2,0:T(8,128)(2,1)}, u32[]{:S(2)}) %copy-start.2) | copy-done | bytes 1146904
  2.0 0.0 copy-start.3
  2.0 1.3 %copy-done.3 = bf16[2,256,1120]{1,2,0:T(8,128)(2,1)S(1)} copy-done((bf16[2,256,1120]{1,2,0:T(8,128)(2,1)S(1)}, bf16[2,256,1120]{1,2,0:T(8,128)(2,1)}, u32[]{:S(2)}) %copy-start.3) | copy-done | bytes 1146904
  3.3 0.0 copy-start.5
  3.3 0.9 %copy-done.5 = f32[9,1120]{1,0:T(8,128)S(1)} copy-done((f32[9,1120]{1,0:T(8,128)S(1)}, f32[9,1120]{1,0:T(8,128)}, u32[]{:S(2)}) %copy-start.5) | copy-done | bytes 40344
  4.1 0.0 copy-start.4
  4.1 0.0 copy-start.6
  4.1 28.4 %states.1 = (f32[3,72,1152]{2,1,0:T(8,128)S(1)}, f32[2,1120,256]{2,1,0:T(8,128)S(1)}) custom-call(bf16[2,1120,256]{2,1,0:T(8,128)(2,1)S(1)} %bitcast.5, bf16[2,1120,256]{2,1,0:T(8,128)(2,1)S(1)} %bitcast.6, f32[9,1120]{1,0:T(8,128)S(1)} %copy-done.5), custom_call_target="tpu_custom_call" | custom-call | tf_op jit(solution)/shard_map/states/pallas_call | solution.py:294
  32.5 0.0 copy-done.1
  32.5 0.0 copy-done.4
  32.6 0.0 copy-done.6
  32.6 0.0 copy-start
  32.6 2.5 %copy-done = bf16[1120,2240]{1,0:T(8,128)(2,1)S(1)} copy-done((bf16[1120,2240]{1,0:T(8,128)(2,1)S(1)}, bf16[1120,2240]{1,0:T(8,128)(2,1)}, u32[]{:S(2)}) %copy-start) | copy-done | bytes 5017624
  35.0 9.2 %project.1 = (f32[2,2240,256]{2,1,0:T(8,128)}, f32[16,70,70]{2,1,0:T(8,128)S(1)}, f32[16,70]{1,0:T(8,128)}) custom-call(s32[2]{0:T(128)S(1)} %copy-done.6, bf16[2,1120,256]{2,1,0:T(8,128)(2,1)S(1)} %bitcast.4, f32[3,72,1152]{2,1,0:T(8,128)S(1)} %get-tuple-element.8.st_ref, f32[2,1120,256]{2,1,0:T(8,128)S(1)} %get-tuple-element.9.conv_ref, ...), custom_call_target="tpu_custom_call" | custom-call | tf_op jit(solution)/shard_map/project/pallas_call | solution.py:328
  44.3 0.9 %copy.10 = f32[16,70,70]{2,0,1:T(8,128)} copy(f32[16,70,70]{2,1,0:T(8,128)S(1)} %get-tuple-element.14) | data formatting | bytes 627200
Async XLA Ops:
  0.6 31.9 %copy-start.1 = (bf16[2,256,1120]{1,2,0:T(8,128)(2,1)S(1)}, bf16[2,256,1120]{1,2,0:T(8,128)(2,1)}, u32[]{:S(2)}) copy-start(bf16[2,256,1120]{1,2,0:T(8,128)(2,1)} %param.7) | copy-start | bytes 3440644
  0.6 1.4 %copy-start.2 = (bf16[2,256,1120]{1,2,0:T(8,128)(2,1)S(1)}, bf16[2,256,1120]{1,2,0:T(8,128)(2,1)}, u32[]{:S(2)}) copy-start(bf16[2,256,1120]{1,2,0:T(8,128)(2,1)} %param.8) | copy-start | bytes 3440644
  2.0 1.3 %copy-start.3 = (bf16[2,256,1120]{1,2,0:T(8,128)(2,1)S(1)}, bf16[2,256,1120]{1,2,0:T(8,128)(2,1)}, u32[]{:S(2)}) copy-start(bf16[2,256,1120]{1,2,0:T(8,128)(2,1)} %param.9) | copy-start | bytes 3440644
  3.3 0.9 %copy-start.5 = (f32[9,1120]{1,0:T(8,128)S(1)}, f32[9,1120]{1,0:T(8,128)}, u32[]{:S(2)}) copy-start(f32[9,1120]{1,0:T(8,128)} %cw_ref.1) | copy-start | bytes 120964
  4.1 28.4 %copy-start.4 = (f32[20,2240]{1,0:T(8,128)S(1)}, f32[20,2240]{1,0:T(8,128)}, u32[]{:S(2)}) copy-start(f32[20,2240]{1,0:T(8,128)} %gate_ref.1) | copy-start | bytes 537604
  4.1 28.4 %copy-start.6 = (s32[2]{0:T(128)S(1)}, s32[2]{0:T(128)}, u32[]{:S(2)}) copy-start(s32[2]{0:T(128)} %ts_ref.1) | copy-start | bytes 28
  32.6 2.5 %copy-start = (bf16[1120,2240]{1,0:T(8,128)(2,1)S(1)}, bf16[1120,2240]{1,0:T(8,128)(2,1)}, u32[]{:S(2)}) copy-start(bf16[1120,2240]{1,0:T(8,128)(2,1)} %w_ref.1) | copy-start | bytes 15052804

commit v3 on v2

--- a/solution.py
+++ b/solution.py
@@ -14,6 +14,9 @@
 LT = 128
 NC = -(-CH // LT)
 NR = 9
+TILES = NR * NC - 1
+SPARE = NC * LT - CH
+EDGE = LT - SPARE
 MESH = pl.DeviceIdType.MESH
 F32 = jnp.float32
 BF16 = jnp.bfloat16
@@ -46,8 +49,12 @@
             rows = band[h * HD - r0 : h * HD - r0 + NR * 8, 0:w]
             tile = jnp.where((lane >= h * HD) & (lane < (h + 1) * HD), rows, tile)
         tile = jnp.where(row < HD, tile, jnp.where(row == HD, count, 0.0))
-        for r in range(NR):
-            put(part, s, r * NC + c, w, tile[8 * r : 8 * r + 8])
+        for r in range(NR - (c == NC - 1)):
+            put(part, s, r * NC + c, slice(0, w), tile[8 * r : 8 * r + 8])
+        if c == NC - 1:
+            for i in range(EDGE // SPARE):
+                piece = tile[8 * NR - 8 :, SPARE * i : SPARE * i + SPARE]
+                put(part, s, i * NC + c, slice(EDGE, LT), piece)
 
 
 def pack(v_ref, lower, out_ref):
@@ -111,9 +118,9 @@
         g, j = idx // m, idx % m
         return g // half, g % half, j
 
-    def put(ref, s, idx, w, value):
+    def put(ref, s, idx, lanes, value):
         c, p, j = place(idx)
-        ref[s, c, p, j, :, 0:w] = value
+        ref[s, c, p, j, :, lanes] = value
 
     barrier = pltpu.get_barrier_semaphore()
     pl.semaphore_signal(barrier, inc=1, device_id={"tm": mate}, device_id_type=MESH)
@@ -220,14 +227,16 @@
         for k in range(half):
             onward(s, k).wait_send()
             onward_in(s, k).wait_recv()
-    for r in range(NR):
-        for c in range(NC):
-            where = place(r * NC + c)
-            rows, cols = slice(8 * r, 8 * r + 8), slice(LT * c, LT * c + LT)
-            whole = full[(0, *where)]
-            st_ref[0, rows, cols] = whole
-            st_ref[1, rows, cols] = whole - part[(0, *where)] + part[(1, *where)]
-            st_ref[2, rows, cols] = full[(1, *where)]
+    for idx in range(TILES):
+        r, c = idx // NC, idx % NC
+        where = place(idx)
+        whole = full[(0, *where)]
+        moved = whole - part[(0, *where)] + part[(1, *where)]
+        for i, tile in enumerate((whole, moved, full[(1, *where)])):
+            st_ref[i, 8 * r : 8 * r + 8, LT * c : LT * c + LT] = tile
+            if c == NC - 1 and r < EDGE // SPARE:
+                lane = LT * c + SPARE * r
+                st_ref[i, 8 * NR - 8 :, lane : lane + SPARE] = tile[:, EDGE:]
 
 
 def split(x):
@@ -288,7 +297,7 @@
     width = out_weight.shape[1]
     half = n // 2
     queries, keys, values = (jnp.swapaxes(x, 1, 2) for x in (queries, keys, values))
-    m = -(-NR * NC // n)
+    m = -(-TILES // n)
     vmem = pl.BlockSpec(memory_space=pltpu.VMEM)
     dma = pltpu.SemaphoreType.DMA
     states, conv = pl.pallas_call(
@@ -321,6 +330,7 @@
         compiler_params=pltpu.CompilerParams(
             collective_id=0, has_side_effects=True, vmem_limit_bytes=20 * 2**20
         ),
+        cost_estimate=pl.CostEstimate(flops=2 * 10**10, bytes_accessed=8 * 10**7, transcendentals=0),
         name="states",
     )(keys, values, conv_weight)
     nb = 640

time: 45.7 us -> 41.2 us (0.902)
  local copies, waits for them, and re-layouts: 6.87 us -> 4.66 us
  Pallas kernels: 37.6 us -> 35.6 us
    unnamed x15 -> x17, local copies, waits for them, and re-layouts: 6.87 us -> 4.66 us
    pallas_call x1, Pallas kernels: 28.4 us -> 26.4 us  [local(): pl.pallas_call(functools.partial(gather_kernel, n, m), out_shape=(jax.Sha...]
where the time goes in v3:
time: 41.2 us; the launch traced here: 41 us
  Pallas kernels  35.6 us (86%)
  local copies, waits for them, and re-layouts  4.66 us (11%)
  between operations  0.71 us (2%)
    pallas_call x1, Pallas kernels, local(): pl.pallas_call(functools.partial(gather_kernel, n, m), out_shape=(jax.Sha...  26.4 us
    pallas_call x1, Pallas kernels, local(): pl.pallas_call(functools.partial(project_kernel, float(tokens * n)), out_...  9.24 us
    unnamed x17, local copies, waits for them, and re-layouts  4.66 us

profile of v3, /device:TPU:0, one launch (start us, length us, event | category | flops | bytes accessed | tf_op | source)
XLA Modules:
  0.0 41.0 jit_solution(10639945082170327784)
XLA Ops:
  0.6 0.0 slice-start
  0.6 0.0 copy-start.3
  0.7 1.4 %copy-done.3 = bf16[2,256,1120]{1,2,0:T(8,128)(2,1)S(1)} copy-done((bf16[2,256,1120]{1,2,0:T(8,128)(2,1)S(1)}, bf16[2,256,1120]{1,2,0:T(8,128)(2,1)}, u32[]{:S(2)}) %copy-start.3) | copy-done | bytes 1146904
  2.1 0.0 copy-start.4
  2.1 1.4 %copy-done.4 = bf16[2,256,1120]{1,2,0:T(8,128)(2,1)S(1)} copy-done((bf16[2,256,1120]{1,2,0:T(8,128)(2,1)S(1)}, bf16[2,256,1120]{1,2,0:T(8,128)(2,1)}, u32[]{:S(2)}) %copy-start.4) | copy-done | bytes 1146904
  3.5 0.0 copy-start.5
  3.5 0.9 %copy-done.5 = f32[9,1120]{1,0:T(8,128)S(1)} copy-done((f32[9,1120]{1,0:T(8,128)S(1)}, f32[9,1120]{1,0:T(8,128)}, u32[]{:S(2)}) %copy-start.5) | copy-done | bytes 40344
  4.4 0.0 slice-start.1
  4.4 0.0 copy-start
  4.4 0.0 copy-start.1
  4.4 0.0 copy-start.2
  4.4 26.4 %states.1 = (f32[3,72,1152]{2,1,0:T(8,128)S(1)}, f32[2,1120,256]{2,1,0:T(8,128)S(1)}) custom-call(bf16[2,1120,256]{2,1,0:T(8,128)(2,1)S(1)} %bitcast.7, bf16[2,1120,256]{2,1,0:T(8,128)(2,1)S(1)} %bitcast.8, f32[9,1120]{1,0:T(8,128)S(1)} %copy-done.5), custom_call_target="tpu_custom_call" | custom-call | flops 20000000000 | bytes 80000000 | tf_op jit(solution)/shard_map/states/pallas_call | solution.py:303
  30.8 0.0 slice-done
  30.8 0.0 slice-done.1
  30.8 0.0 copy-done
  30.8 0.0 copy-done.1
  30.8 0.0 copy-done.2
  30.9 9.2 %project.1 = (f32[2,2240,256]{2,1,0:T(8,128)}, f32[16,70,70]{2,1,0:T(8,128)S(1)}, f32[16,70]{1,0:T(8,128)}) custom-call(s32[2]{0:T(128)S(1)} %copy-done.2, bf16[2,1120,256]{2,1,0:T(8,128)(2,1)S(1)} %bitcast.6, f32[3,72,1152]{2,1,0:T(8,128)S(1)} %get-tuple-element.8.st_ref, f32[2,1120,256]{2,1,0:T(8,128)S(1)} %get-tuple-element.9.conv_ref, ...), custom_call_target="tpu_custom_call" | custom-call | tf_op jit(solution)/shard_map/project/pallas_call | solution.py:338
  40.1 0.9 %copy.10 = f32[16,70,70]{2,0,1:T(8,128)} copy(f32[16,70,70]{2,1,0:T(8,128)S(1)} %get-tuple-element.14) | data formatting | bytes 627200
  (1 shorter events, 0.0 us)
Async XLA Ops:
  0.6 30.2 %slice-start = ((s8[5160960]{0:T(1024)(128)(4,1)}), s8[4194304]{0:T(1024)(128)(4,1)S(1)}, s32[]{:S(2)}) async-start(s8[5160960]{0:T(1024)(128)(4,1)} %bitcast.4), calls=%async_computation | async-start | bytes 8388608
  0.6 1.4 %copy-start.3 = (bf16[2,256,1120]{1,2,0:T(8,128)(2,1)S(1)}, bf16[2,256,1120]{1,2,0:T(8,128)(2,1)}, u32[]{:S(2)}) copy-start(bf16[2,256,1120]{1,2,0:T(8,128)(2,1)} %param.8) | copy-start | bytes 3440644
  2.1 1.4 %copy-start.4 = (bf16[2,256,1120]{1,2,0:T(8,128)(2,1)S(1)}, bf16[2,256,1120]{1,2,0:T(8,128)(2,1)}, u32[]{:S(2)}) copy-start(bf16[2,256,1120]{1,2,0:T(8,128)(2,1)} %param.9) | copy-start | bytes 3440644
  3.5 0.9 %copy-start.5 = (f32[9,1120]{1,0:T(8,128)S(1)}, f32[9,1120]{1,0:T(8,128)}, u32[]{:S(2)}) copy-start(f32[9,1120]{1,0:T(8,128)} %cw_ref.1) | copy-start | bytes 120964
  4.4 26.4 %slice-start.1 = ((s8[5160960]{0:T(1024)(128)(4,1)}), s8[966656]{0:T(1024)(128)(4,1)S(1)}, s32[]{:S(2)}) async-start(s8[5160960]{0:T(1024)(128)(4,1)} %bitcast.4), calls=%async_computation.1 | async-start | bytes 1933312
  4.4 26.4 %copy-start = (bf16[2,256,1120]{1,2,0:T(8,128)(2,1)S(1)}, bf16[2,256,1120]{1,2,0:T(8,128)(2,1)}, u32[]{:S(2)}) copy-start(bf16[2,256,1120]{1,2,0:T(8,128)(2,1)} %param.7) | copy-start | bytes 3440644
  4.4 26.4 %copy-start.1 = (f32[20,2240]{1,0:T(8,128)S(1)}, f32[20,2240]{1,0:T(8,128)}, u32[]{:S(2)}) copy-start(f32[20,2240]{1,0:T(8,128)} %gate_ref.1) | copy-start | bytes 537604
  4.4 26.5 %copy-start.2 = (s32[2]{0:T(128)S(1)}, s32[2]{0:T(128)}, u32[]{:S(2)}) copy-start(s32[2]{0:T(128)} %ts_ref.1) | copy-start | bytes 28

commit v4 on v3

--- a/solution.py
+++ b/solution.py
@@ -101,7 +101,8 @@
 
 
 def gather_kernel(
-    n, m, k_ref, v_ref, cw_ref, st_ref, conv_ref,
+    n, m, k_hbm, v_hbm, cw_ref, st_ref, conv_ref,
+    k_ref, v_ref, in_sem,
     part, cin, cur, rin, full, edge, rim, above, below, wide, taps, band,
     core_s, core_r, p1_s, p1_r, p2_s, p2_r, fw_s, fw_r, rim_s, rim_r,
 ):
@@ -122,6 +123,13 @@
         c, p, j = place(idx)
         ref[s, c, p, j, :, lanes] = value
 
+    def fetch(i, s):
+        src, dst = ((k_hbm, k_ref), (v_hbm, v_ref))[i]
+        return pltpu.make_async_copy(src.at[s], dst.at[s], in_sem.at[i, s])
+
+    for s in range(2):
+        for i in range(2):
+            fetch(i, s).start()
     barrier = pltpu.get_barrier_semaphore()
     pl.semaphore_signal(barrier, inc=1, device_id={"tm": mate}, device_id_type=MESH)
     for k in range(1, half):
@@ -162,6 +170,8 @@
     up = remote(edge.at[1], rim.at[1], rim_s.at[1], rim_r.at[1], me - 1)
 
     part[...] = jnp.zeros_like(part)
+    for i in range(2):
+        fetch(i, 0).wait()
     local_state(k_ref, v_ref, 0, part, band, put)
     swap(0).start()
     pack(v_ref, True, edge.at[0])
@@ -175,6 +185,8 @@
     def _():
         up.start()
 
+    for i in range(2):
+        fetch(i, 1).wait()
     local_state(k_ref, v_ref, 1, part, band, put)
     swap(1).start()
     wide[...] = jnp.zeros_like(wide)
@@ -306,9 +318,12 @@
             jax.ShapeDtypeStruct((3, NR * 8, NC * LT), F32),
             jax.ShapeDtypeStruct((2, CH, tokens), F32),
         ),
-        in_specs=[vmem] * 3,
+        in_specs=[pl.BlockSpec(memory_space=pltpu.MemorySpace.HBM)] * 2 + [vmem],
         out_specs=(vmem, vmem),
         scratch_shapes=[
+            pltpu.VMEM((2, CH, tokens), BF16),
+            pltpu.VMEM((2, CH, tokens), BF16),
+            dma((2, 2)),
             pltpu.VMEM((2, 2, half, m, 8, LT), F32),
             pltpu.VMEM((2, half, m, 8, LT), F32),
             pltpu.VMEM((2, half, m, 8, LT), F32),

time: 41.2 us -> 41.7 us (1.012)
  Pallas kernels: 35.6 us -> 36.1 us
    pallas_call x1, Pallas kernels: 26.4 us -> 26.9 us  [local(): pl.pallas_call(functools.partial(gather_kernel, n, m), out_shape=(jax.Sha...]
where the time goes in v4:
time: 41.7 us; the launch traced here: 41.5 us
  Pallas kernels  36.1 us (87%)
  local copies, waits for them, and re-layouts  4.66 us (11%)
  between operations  0.71 us (2%)
    pallas_call x1, Pallas kernels, local(): pl.pallas_call(functools.partial(gather_kernel, n, m), out_shape=(jax.Sha...  26.9 us
    pallas_call x1, Pallas kernels, local(): pl.pallas_call(functools.partial(project_kernel, float(tokens * n)), out_...  9.24 us
    unnamed x17, local copies, waits for them, and re-layouts  4.66 us

profile of v4, /device:TPU:0, one launch (start us, length us, event | category | flops | bytes accessed | tf_op | source)
XLA Modules:
  0.0 41.5 jit_solution(18124961315300808969)
XLA Ops:
  0.6 0.0 slice-start
  0.6 0.0 copy-start.3
  0.7 1.4 %copy-done.3 = bf16[2,256,1120]{1,2,0:T(8,128)(2,1)S(1)} copy-done((bf16[2,256,1120]{1,2,0:T(8,128)(2,1)S(1)}, bf16[2,256,1120]{1,2,0:T(8,128)(2,1)}, u32[]{:S(2)}) %copy-start.3) | copy-done | bytes 1146904
  2.1 0.0 copy-start.4
  2.1 1.4 %copy-done.4 = bf16[2,256,1120]{1,2,0:T(8,128)(2,1)S(1)} copy-done((bf16[2,256,1120]{1,2,0:T(8,128)(2,1)S(1)}, bf16[2,256,1120]{1,2,0:T(8,128)(2,1)}, u32[]{:S(2)}) %copy-start.4) | copy-done | bytes 1146904
  3.5 0.0 copy-start.5
  3.5 0.9 %copy-done.5 = f32[9,1120]{1,0:T(8,128)S(1)} copy-done((f32[9,1120]{1,0:T(8,128)S(1)}, f32[9,1120]{1,0:T(8,128)}, u32[]{:S(2)}) %copy-start.5) | copy-done | bytes 40344
  4.4 0.0 slice-start.1
  4.4 0.0 copy-start
  4.4 0.0 copy-start.1
  4.4 0.0 copy-start.2
  4.4 26.9 %states.1 = (f32[3,72,1152]{2,1,0:T(8,128)S(1)}, f32[2,1120,256]{2,1,0:T(8,128)S(1)}) custom-call(bf16[2,1120,256]{2,1,0:T(8,128)(2,1)S(1)} %bitcast.7, bf16[2,1120,256]{2,1,0:T(8,128)(2,1)S(1)} %bitcast.8, f32[9,1120]{1,0:T(8,128)S(1)} %copy-done.5), custom_call_target="tpu_custom_call" | custom-call | flops 20000000000 | bytes 80000000 | tf_op jit(solution)/shard_map/states/pallas_call | solution.py:315
  31.3 0.0 slice-done
  31.3 0.0 slice-done.1
  31.3 0.0 copy-done
  31.3 0.0 copy-done.1
  31.3 0.0 copy-done.2
  31.4 9.2 %project.1 = (f32[2,2240,256]{2,1,0:T(8,128)}, f32[16,70,70]{2,1,0:T(8,128)S(1)}, f32[16,70]{1,0:T(8,128)}) custom-call(s32[2]{0:T(128)S(1)} %copy-done.2, bf16[2,1120,256]{2,1,0:T(8,128)(2,1)S(1)} %bitcast.6, f32[3,72,1152]{2,1,0:T(8,128)S(1)} %get-tuple-element.8.st_ref, f32[2,1120,256]{2,1,0:T(8,128)S(1)} %get-tuple-element.9.conv_ref, ...), custom_call_target="tpu_custom_call" | custom-call | tf_op jit(solution)/shard_map/project/pallas_call | solution.py:353
  40.6 0.9 %copy.10 = f32[16,70,70]{2,0,1:T(8,128)} copy(f32[16,70,70]{2,1,0:T(8,128)S(1)} %get-tuple-element.14) | data formatting | bytes 627200
  (1 shorter events, 0.0 us)
Async XLA Ops:
  0.6 30.7 %slice-start = ((s8[5160960]{0:T(1024)(128)(4,1)}), s8[4194304]{0:T(1024)(128)(4,1)S(1)}, s32[]{:S(2)}) async-start(s8[5160960]{0:T(1024)(128)(4,1)} %bitcast.4), calls=%async_computation | async-start | bytes 8388608
  0.6 1.4 %copy-start.3 = (bf16[2,256,1120]{1,2,0:T(8,128)(2,1)S(1)}, bf16[2,256,1120]{1,2,0:T(8,128)(2,1)}, u32[]{:S(2)}) copy-start(bf16[2,256,1120]{1,2,0:T(8,128)(2,1)} %param.8) | copy-start | bytes 3440644
  2.1 1.4 %copy-start.4 = (bf16[2,256,1120]{1,2,0:T(8,128)(2,1)S(1)}, bf16[2,256,1120]{1,2,0:T(8,128)(2,1)}, u32[]{:S(2)}) copy-start(bf16[2,256,1120]{1,2,0:T(8,128)(2,1)} %param.9) | copy-start | bytes 3440644
  3.5 0.9 %copy-start.5 = (f32[9,1120]{1,0:T(8,128)S(1)}, f32[9,1120]{1,0:T(8,128)}, u32[]{:S(2)}) copy-start(f32[9,1120]{1,0:T(8,128)} %cw_ref.1) | copy-start | bytes 120964
  4.4 26.9 %slice-start.1 = ((s8[5160960]{0:T(1024)(128)(4,1)}), s8[966656]{0:T(1024)(128)(4,1)S(1)}, s32[]{:S(2)}) async-start(s8[5160960]{0:T(1024)(128)(4,1)} %bitcast.4), calls=%async_computation.1 | async-start | bytes 1933312
  4.4 26.9 %copy-start = (bf16[2,256,1120]{1,2,0:T(8,128)(2,1)S(1)}, bf16[2,256,1120]{1,2,0:T(8,128)(2,1)}, u32[]{:S(2)}) copy-start(bf16[2,256,1120]{1,2,0:T(8,128)(2,1)} %param.7) | copy-start | bytes 3440644
  4.4 26.9 %copy-start.1 = (f32[20,2240]{1,0:T(8,128)S(1)}, f32[20,2240]{1,0:T(8,128)}, u32[]{:S(2)}) copy-start(f32[20,2240]{1,0:T(8,128)} %gate_ref.1) | copy-start | bytes 537604
  4.4 27.0 %copy-start.2 = (s32[2]{0:T(128)S(1)}, s32[2]{0:T(128)}, u32[]{:S(2)}) copy-start(s32[2]{0:T(128)} %ts_ref.1) | copy-start | bytes 28
